TPU v7x, 512 devices: a whole 4x8x8 slice. The times are simulated.
512 devices in a mesh: dp: 8 (over y), expert: 64 (over z, x, core).
Axes of the slice: x: 4, y: 8, z: 8, core: 2. Of those that a mesh axis runs over, the one named last changes fastest.
Arguments:
- tokens: bfloat16 [4096, 4096], P('expert', 'dp'), may hold values from -6 to 6
- expert_ids: int32 [4096, 8], P('expert'), may hold values from 0 to 63, all different within a row; in each aligned block of 64 rows (0 to 63, 64 to 127, ...) at most 16 rows name the same one
- gate_weights: float32 [4096, 8], P('expert'), may hold values from 0.05 to 1
- gate_proj: bfloat16 [64, 4096, 1536], P('expert', 'dp'), may hold values from -0.09375 to 0.09375
- up_proj: bfloat16 [64, 4096, 1536], P('expert', 'dp'), may hold values from -0.09375 to 0.09375
- down_proj: bfloat16 [64, 1536, 4096], P('expert', None, 'dp'), may hold values from -0.15625 to 0.15625
Outputs:
- combined: bfloat16 [4096, 4096], P('expert', 'dp')
Inputs may be any that keep to these rules, and one draw needn't show every extreme that they name: `expert_ids`: each row names 8 different experts. Among the 64 rows of one device (one aligned block), no expert is named by more than 16 rows, and in every draw some expert is named by exactly 16 rows of some block.
All inputs are finite; a program needn't handle non-finite values.
Results may differ from a plain program's by a relative error of at most 0.029.
Values may be sent and summed in bfloat16 or wider, within the bound.
A program may use at most 64 MiB of HBM per device.

v0:
```python
import jax
import jax.numpy as jnp
from jax import lax
from jax.sharding import PartitionSpec as P


def block_places(block_ids, expert_count, capacity):
    tok_count, top_count = block_ids.shape
    flat_ids = block_ids.reshape(tok_count * top_count)
    matches = (flat_ids[:, None] == jnp.arange(expert_count, dtype=jnp.int32)[None, :]).astype(
        jnp.int32
    )
    earlier = jnp.cumsum(matches, axis=0) - matches
    slot_index = jnp.sum(earlier * matches, axis=1)
    return (flat_ids * capacity + slot_index).reshape(tok_count, top_count)


def body(tokens, expert_ids, gate_weights, gate_proj, up_proj, down_proj):
    tok_count, top_count = expert_ids.shape
    row_width = tokens.shape[1]
    sources = lax.axis_size("expert")
    capacity = 2 * tok_count * top_count // sources
    positions = jnp.arange(sources * capacity, dtype=jnp.int32)
    places = block_places(expert_ids, sources, capacity)
    matches = places[:, :, None] == positions[None, None, :]
    weighting = jnp.sum(jnp.where(matches, gate_weights[:, :, None], 0.0), axis=1)
    chosen = jnp.any(matches, axis=1).astype(jnp.bfloat16)
    outgoing = lax.dot_general(
        chosen, tokens, (((0,), (0,)), ((), ())), preferred_element_type=jnp.float32
    ).astype(jnp.bfloat16)
    incoming = lax.all_to_all(
        outgoing.reshape(sources, capacity, row_width),
        "expert",
        split_axis=0,
        concat_axis=0,
        tiled=True,
    )
    expert_rows = incoming.reshape(sources * capacity, row_width)
    gate_part = jnp.dot(expert_rows, gate_proj[0], preferred_element_type=jnp.float32)
    up_part = jnp.dot(expert_rows, up_proj[0], preferred_element_type=jnp.float32)
    gate_sum, up_sum = (
        lax.psum(gate_part.astype(jnp.bfloat16), "dp").astype(jnp.float32),
        lax.psum(up_part.astype(jnp.bfloat16), "dp").astype(jnp.float32),
    )
    hidden = (jax.nn.silu(gate_sum) * up_sum).astype(jnp.bfloat16)
    expert_out = jnp.dot(hidden, down_proj[0], preferred_element_type=jnp.float32).astype(
        jnp.bfloat16
    )
    returned = lax.all_to_all(
        expert_out.reshape(sources, capacity, row_width),
        "expert",
        split_axis=0,
        concat_axis=0,
        tiled=True,
    )
    returned_flat = returned.reshape(sources * capacity, row_width)
    weight_high = weighting.astype(jnp.bfloat16)
    weight_low = (weighting - weight_high.astype(jnp.float32)).astype(jnp.bfloat16)
    combined = jnp.dot(weight_high, returned_flat, preferred_element_type=jnp.float32)
    combined = combined + jnp.dot(weight_low, returned_flat, preferred_element_type=jnp.float32)
    return combined.astype(jnp.bfloat16)


def solution(mesh):
    placed = (
        P("expert", "dp"),
        P("expert", None),
        P("expert", None),
        P("expert", "dp", None),
        P("expert", "dp", None),
        P("expert", None, "dp"),
    )
    return jax.shard_map(
        body, mesh=mesh, in_specs=placed, out_specs=P("expert", "dp"), check_vma=False
    )
```

profile of v0, /device:TPU:1, one launch (start us, length us, event | category | flops | bytes accessed | tf_op | source)
XLA Modules:
  0.0 266.4 jit_solution(7959144195242189206)
XLA Ops:
  6.5 0.9 copy.21
  7.4 0.1 eq.42
  7.5 0.1 eq.38
  7.6 1.2 reduce-window.6
  8.8 0.2 slice_reduce_fusion
  9.1 0.1 fusion.19
  9.2 0.1 reduce_sum.21
  9.3 0.1 copy.24
  9.4 0.7 multiply_add_fusion
  10.1 0.1 copy.25
  10.2 0.7 fusion.7
  10.9 1.3 convolution_convert_fusion.2
  12.2 42.6 %all_to_all.10 = bf16[64,16,512]{2,1,0:T(8,128)(2,1)S(1)} all-to-all(bf16[64,16,512]{2,1,0:T(8,128)(2,1)S(1)} %bitcast.42), channel_id=1, replica_groups=mesh['dp'=8,'expert'=64] {'expert'}, dimensions={0} | all-to-all | bytes 2097152 | tf_op jit(solution)/shard_map/all_to_all | solution.py:31
  54.8 3.5 %convolution_convert_fusion = bf16[1024,1536]{1,0:T(8,128)(2,1)} fusion(bf16[1024,512]{1,0:T(8,128)(2,1)S(1)} %bitcast.44, bf16[1,512,1536]{2,1,0:T(8,128)(2,1)S(1)} %copy-done), kind=kOutput, calls=%fused_computation.7 | convolution fusion | flops 1612185600 | bytes 5767168 | tf_op jit(solution)/shard_map/dot_general | solution.py:40
  58.3 3.4 %convolution_convert_fusion.1 = bf16[1024,1536]{1,0:T(8,128)(2,1)} fusion(bf16[1024,512]{1,0:T(8,128)(2,1)S(1)} %bitcast.45, bf16[1,512,1536]{2,1,0:T(8,128)(2,1)S(1)} %copy-done.2), kind=kOutput, calls=%fused_computation.8 | convolution fusion | flops 1612185600 | bytes 5767168 | tf_op jit(solution)/shard_map/dot_general | solution.py:39
  61.8 0.0 all-reduce.3.cloned.1.call-update
  61.8 151.3 %all-reduce.3.cloned.1.call-done = (bf16[1024,1536]{1,0:T(8,128)(2,1)}, bf16[1024,1536]{1,0:T(8,128)(2,1)}) async-done(((bf16[1024,1536]{1,0:T(8,128)(2,1)}, bf16[1024,1536]{1,0:T(8,128)(2,1)}), (bf16[1024,1536]{1,0:T(8,128)(2,1)}, bf16[1024,1536]{1,0:T(8,128)(2,1)})) %all-reduce.3.cloned.1.call-update) | async-done | bytes 6291472 | tf_op jit(solution)/shard_map/psum | solution.py:43
  213.1 6.2 %fusion.11 = bf16[1024,512]{1,0:T(8,128)(2,1)} fusion(bf16[1,1536,512]{2,1,0:T(8,128)(2,1)} %param.11, bf16[1024,1536]{1,0:T(8,128)(2,1)} %get-tuple-element.5, bf16[1024,1536]{1,0:T(8,128)(2,1)} %get-tuple-element.6), kind=kOutput, calls=%fused_computation.16 | convolution fusion | flops 1623719936 | bytes 8912896 | tf_op jit(solution)/shard_map/dot_general | solution.py:46
  219.3 11.0 %all-to-all-start.1 = ((bf16[64,16,512]{2,1,0:T(8,128)(2,1)}), bf16[64,16,512]{2,1,0:T(8,128)(2,1)S(1)}, u32[]{:S(2)}, u32[]{:S(2)}) async-start(bf16[64,16,512]{2,1,0:T(8,128)(2,1)} %bitcast.43), calls=%async_computation.1 | async-start | bytes 2097152 | tf_op jit(solution)/shard_map/all_to_all | solution.py:49
  230.4 0.1 copy.26
  230.5 0.7 select_reduce_fusion
  231.2 27.2 %all-to-all-done.1 = bf16[64,16,512]{2,1,0:T(8,128)(2,1)S(1)} async-done(((bf16[64,16,512]{2,1,0:T(8,128)(2,1)}), bf16[64,16,512]{2,1,0:T(8,128)(2,1)S(1)}, u32[]{:S(2)}, u32[]{:S(2)}) %all-to-all-start.1) | async-done | bytes 1048608 | tf_op jit(solution)/shard_map/all_to_all | solution.py:49
  258.3 0.3 fusion.22
  258.6 0.9 fusion.16
  (10 shorter events, 0.1 us)
Async XLA Ops:
  6.5 48.3 %copy-start = (bf16[1,512,1536]{2,1,0:T(8,128)(2,1)S(1)}, bf16[1,512,1536]{2,1,0:T(8,128)(2,1)}, u32[]{:S(2)}) copy-start(bf16[1,512,1536]{2,1,0:T(8,128)(2,1)} %param.10) | copy-start | bytes 4718596
  6.5 206.6 %all-reduce.3.cloned.1.call-start = ((), (), s32[]{:S(2)}) async-start(), calls=%async_computation.2 | async-start | bytes 12582912 | tf_op jit(solution)/shard_map/psum | solution.py:43
  54.8 3.5 %copy-start.2 = (bf16[1,512,1536]{2,1,0:T(8,128)(2,1)S(1)}, bf16[1,512,1536]{2,1,0:T(8,128)(2,1)}, u32[]{:S(2)}) copy-start(bf16[1,512,1536]{2,1,0:T(8,128)(2,1)} %param.9) | copy-start | bytes 4718596
  213.1 17.3 %copy-start.1 = (f32[64,8]{0,1:T(8,128)S(1)}, f32[64,8]{0,1:T(8,128)}, u32[]{:S(2)}) copy-start(f32[64,8]{0,1:T(8,128)} %param.8) | copy-start | bytes 6148
  219.3 39.0 %all-to-all-start.1 = ((bf16[64,16,512]{2,1,0:T(8,128)(2,1)}), bf16[64,16,512]{2,1,0:T(8,128)(2,1)S(1)}, u32[]{:S(2)}, u32[]{:S(2)}) async-start(bf16[64,16,512]{2,1,0:T(8,128)(2,1)} %bitcast.43), calls=%async_computation.1 | async-start | bytes 2097152 | tf_op jit(solution)/shard_map/all_to_all | solution.py:49
Sparse Core Ops, SparseCore 0:
  61.9 151.1 all-reduce.2
where the time goes:
time: 267 us; the launch traced here: 266 us
  waiting for transfers between devices  178 us (67%)
  blocking collectives  42.6 us (16%)
  matrix products  15.7 us (6%)
  between operations  13.5 us (5%)
  starting transfers between devices  11 us (4%)
  other arithmetic  3.49 us (1%)
    psum x1, waiting for transfers between devices, body(): lax.psum(up_part.astype(jnp.bfloat16), 'dp').astype(jnp.float32)  151 us
    all_to_all x1, blocking collectives, body(): lax.all_to_all(outgoing.reshape(sources, capacity, row_width), 'expert',...  42.6 us
    all_to_all x1, waiting for transfers between devices, body(): lax.all_to_all(expert_out.reshape(sources, capacity, row_width), 'expert'...  27.2 us
    all_to_all x1, starting transfers between devices, body(): lax.all_to_all(expert_out.reshape(sources, capacity, row_width), 'expert'...  11 us
    dot_general x1, matrix products, body(): jnp.dot(hidden, down_proj[0], preferred_element_type=jnp.float32)  6.23 us
  transfers between devices with their start and end apart: 2, of which 2 were waited for; matrix products, arithmetic and copies ran while one was open for 0% of the time, Pallas kernels for 0%

commit v1 on v0

--- a/solution.py
+++ b/solution.py
@@ -2,6 +2,7 @@
 import jax.numpy as jnp
 from jax import lax
 from jax.sharding import PartitionSpec as P
+from jax.lax import all_gather
 
 
 def block_places(block_ids, expert_count, capacity):
@@ -40,7 +41,7 @@
     up_part = jnp.dot(expert_rows, up_proj[0], preferred_element_type=jnp.float32)
     gate_sum, up_sum = (
         lax.psum(gate_part.astype(jnp.bfloat16), "dp").astype(jnp.float32),
-        lax.psum(up_part.astype(jnp.bfloat16), "dp").astype(jnp.float32),
+        jnp.sum(all_gather(up_part.astype(jnp.bfloat16), axis_name="dp"), 0).astype(jnp.float32),
     )
     hidden = (jax.nn.silu(gate_sum) * up_sum).astype(jnp.bfloat16)
     expert_out = jnp.dot(hidden, down_proj[0], preferred_element_type=jnp.float32).astype(

time: 267 us -> 461 us (1.73)
  waiting for transfers between devices: 178 us -> 355 us
  other arithmetic: 3.49 us -> 19 us
    all_gather x0 -> x1, waiting for transfers between devices: none -> 246 us  [body(): all_gather(up_part.astype(jnp.bfloat16), axis_name='dp')]
    psum x1, waiting for transfers between devices: 151 us -> 81.7 us  [body(): lax.psum(gate_part.astype(jnp.bfloat16), 'dp').astype(jnp.float32)]
    reduce_sum x0 -> x1, other arithmetic: none -> 15.6 us  [body(): jnp.sum(all_gather(up_part.astype(jnp.bfloat16), axis_name='dp'), 0)]
  transfers between devices with their start and end apart: 2 -> 3, of which waited for: 2 -> 3; matrix products, arithmetic and copies ran while one was open for 0% -> 5% of each run, Pallas kernels for 0% -> 0%
where the time goes in v1:
time: 461 us
  waiting for transfers between devices  355 us (77%)
  blocking collectives  42.6 us (9%)
  other arithmetic  19 us (4%)
  matrix products  17.1 us (4%)
  between operations  13.5 us (3%)
  starting transfers between devices  11.9 us (3%)
    all_gather x1, waiting for transfers between devices, body(): all_gather(up_part.astype(jnp.bfloat16), axis_name='dp')  246 us
    psum x1, waiting for transfers between devices, body(): lax.psum(gate_part.astype(jnp.bfloat16), 'dp').astype(jnp.float32)  81.7 us
    all_to_all x1, blocking collectives, body(): lax.all_to_all(outgoing.reshape(sources, capacity, row_width), 'expert',...  42.6 us
    all_to_all x1, waiting for transfers between devices, body(): lax.all_to_all(expert_out.reshape(sources, capacity, row_width), 'expert'...  27.2 us
    reduce_sum x1, other arithmetic, body(): jnp.sum(all_gather(up_part.astype(jnp.bfloat16), axis_name='dp'), 0)  15.6 us
    all_to_all x1, starting transfers between devices, body(): lax.all_to_all(expert_out.reshape(sources, capacity, row_width), 'expert'...  11.9 us
  transfers between devices with their start and end apart: 3, of which 3 were waited for; matrix products, arithmetic and copies ran while one was open for 5% of the time, Pallas kernels for 0%

profile of v1, /device:TPU:1, one launch (start us, length us, event | category | flops | bytes accessed | tf_op | source)
XLA Modules:
  0.0 460.8 jit_solution(11014268018112297982)
XLA Ops:
  6.5 0.9 copy.21
  7.4 0.1 eq.42
  7.5 0.1 eq.38
  7.6 1.2 reduce-window.6
  8.8 0.2 slice_reduce_fusion
  9.1 0.1 fusion.19
  9.2 0.1 reduce_sum.33
  9.4 0.7 multiply_add_fusion
  10.1 0.1 copy.25
  10.2 0.7 fusion.7
  10.9 1.3 convolution_convert_fusion.2
  12.2 42.6 %all_to_all.10 = bf16[64,16,512]{2,1,0:T(8,128)(2,1)S(1)} all-to-all(bf16[64,16,512]{2,1,0:T(8,128)(2,1)S(1)} %bitcast.44), channel_id=1, replica_groups=mesh['dp'=8,'expert'=64] {'expert'}, dimensions={0} | all-to-all | bytes 2097152 | tf_op jit(solution)/shard_map/all_to_all | solution.py:32
  54.8 3.5 convolution_convert_fusion
  58.5 4.8 %convolution_convert_fusion.1 = bf16[1024,1536]{1,0:T(8,128)(2,1)} fusion(bf16[1024,512]{1,0:T(8,128)(2,1)S(1)} %bitcast.46, bf16[1,512,1536]{2,1,0:T(8,128)(2,1)} %param.9), kind=kOutput, calls=%fused_computation.8 | convolution fusion | flops 1612185600 | bytes 5767168 | tf_op jit(solution)/shard_map/dot_general | solution.py:40
  63.3 246.1 %all-gather.3.cloned.1.call-done = bf16[8192,1536]{1,0:T(8,128)(2,1)} async-done(((bf16[1024,1536]{1,0:T(8,128)(2,1)}), bf16[8192,1536]{1,0:T(8,128)(2,1)}) %all-gather.3.cloned.1.call-update) | async-done | bytes 25165840 | tf_op jit(solution)/shard_map/all_gather | solution.py:44
  309.4 15.6 %reduce_sum.35 = bf16[1024,1536]{1,0:T(8,128)(2,1)} reduce(bf16[8,1024,1536]{2,1,0:T(8,128)(2,1)} %bitcast.41, bf16[]{:T(256)} %constant.16.clone.1), dimensions={0}, to_apply=%region_6.7 | reduce | flops 11010048 | bytes 28311554 | tf_op jit(solution)/shard_map/reduce_sum | solution.py:44
  324.9 81.7 %all-reduce.2.cloned.1.call-done = bf16[1024,1536]{1,0:T(8,128)(2,1)} async-done(((bf16[1024,1536]{1,0:T(8,128)(2,1)}), bf16[1024,1536]{1,0:T(8,128)(2,1)}) %all-reduce.2.cloned.1.call-update) | async-done | bytes 3145744 | tf_op jit(solution)/shard_map/psum | solution.py:43
  406.7 6.2 %fusion.11 = bf16[1024,512]{1,0:T(8,128)(2,1)} fusion(bf16[1,1536,512]{2,1,0:T(8,128)(2,1)} %param.11, bf16[1024,1536]{1,0:T(8,128)(2,1)} %reduce_sum.35, bf16[1024,1536]{1,0:T(8,128)(2,1)} %all-reduce.2.cloned.1.call-done), kind=kOutput, calls=%fused_computation.16 | convolution fusion | flops 1623719936 | bytes 8912896 | tf_op jit(solution)/shard_map/dot_general | solution.py:47
  412.9 11.9 %all-to-all-start.1 = ((bf16[64,16,512]{2,1,0:T(8,128)(2,1)}), bf16[64,16,512]{2,1,0:T(8,128)(2,1)S(1)}, u32[]{:S(2)}, u32[]{:S(2)}) async-start(bf16[64,16,512]{2,1,0:T(8,128)(2,1)} %bitcast.47), calls=%async_computation.1 | async-start | bytes 2097152 | tf_op jit(solution)/shard_map/all_to_all | solution.py:50
  424.8 0.1 copy.26
  424.8 0.7 select_reduce_fusion
  425.6 27.2 %all-to-all-done.1 = bf16[64,16,512]{2,1,0:T(8,128)(2,1)S(1)} async-done(((bf16[64,16,512]{2,1,0:T(8,128)(2,1)}), bf16[64,16,512]{2,1,0:T(8,128)(2,1)S(1)}, u32[]{:S(2)}, u32[]{:S(2)}) %all-to-all-start.1) | async-done | bytes 1048608 | tf_op jit(solution)/shard_map/all_to_all | solution.py:50
  452.7 0.3 fusion.22
  453.0 0.9 fusion.16
  (12 shorter events, 0.2 us)
Async XLA Ops:
  6.5 48.3 %copy-start = (bf16[1,512,1536]{2,1,0:T(8,128)(2,1)S(1)}, bf16[1,512,1536]{2,1,0:T(8,128)(2,1)}, u32[]{:S(2)}) copy-start(bf16[1,512,1536]{2,1,0:T(8,128)(2,1)} %param.10) | copy-start | bytes 4718596
  6.5 302.9 %all-gather.3.cloned.1.call-start = ((), (), s32[]{:S(2)}) async-start(), calls=%async_computation.3 | async-start | bytes 28311552 | tf_op jit(solution)/shard_map/all_gather | solution.py:44
  58.4 348.3 %all-reduce.2.cloned.1.call-start = ((), (), s32[]{:S(2)}) async-start(), calls=%async_computation.2 | async-start | bytes 6291456 | tf_op jit(solution)/shard_map/psum | solution.py:43
  324.9 99.8 %copy-start.1 = (f32[64,8]{0,1:T(8,128)S(1)}, f32[64,8]{0,1:T(8,128)}, u32[]{:S(2)}) copy-start(f32[64,8]{0,1:T(8,128)} %param.8) | copy-start | bytes 6148
  412.9 39.9 %all-to-all-start.1 = ((bf16[64,16,512]{2,1,0:T(8,128)(2,1)}), bf16[64,16,512]{2,1,0:T(8,128)(2,1)S(1)}, u32[]{:S(2)}, u32[]{:S(2)}) async-start(bf16[64,16,512]{2,1,0:T(8,128)(2,1)} %bitcast.47), calls=%async_computation.1 | async-start | bytes 2097152 | tf_op jit(solution)/shard_map/all_to_all | solution.py:50
Sparse Core Ops, SparseCore 0:
  58.5 250.8 all-gather.2
  311.8 94.8 all-reduce.1
